TPU v7x, 128 devices: a whole 4x4x4 slice. The times are simulated.
128 devices in a mesh: row: 8 (over z, core), col: 16 (over x, y).
Axes of the slice: x: 4, y: 4, z: 4, core: 2. Of those that a mesh axis runs over, the one named last changes fastest.
Arguments:
- embed: bfloat16 [262144, 64], P(('row', 'col')), may hold values from -6 to 6
- tiles: bfloat16 [8192, 128, 128], P(('row', 'col'))
- tile_rows: int32 [8192], P(('row', 'col')), may hold values from 0 to 2047, as said below
- tile_cols: int32 [8192], P(('row', 'col')), may hold values from 0 to 2047, as said below
- chg_tiles: bfloat16 [24576, 128, 128], P(('row', 'col'))
- chg_rows: int32 [24576], P(('row', 'col')), may hold values from 0 to 2047, as said below
- chg_cols: int32 [24576], P(('row', 'col')), may hold values from 0 to 2047, as said below
Outputs:
- embedding: float32 [262144, 64], P(('row', 'col'))
Inputs may be any that keep to these rules, and one draw needn't show every extreme that they name: Tile n lies in the row group of the device that holds it: tile_rows[n] // 256 equals (n // 64) // 16. Tile n lies in the column group of the device that holds it: tile_cols[n] // 128 equals (n // 64) % 16. `chg_rows`: one device's list names each transpose owner at most 3 times; in every draw some owner is named exactly 3 times by every device's list. `chg_cols`: read with chg_rows to give the transpose owner.
All inputs are finite; a program needn't handle non-finite values.
Results may differ from a plain program's by a relative error of at most 0.025.
Values may be sent and summed in bfloat16 or wider, within the bound.
A program may use at most 192 MiB of HBM per device.

v0:
```python
import jax
import jax.numpy as jnp
from jax import lax
from jax.sharding import PartitionSpec as P

ITERS = 3
CAP = 3


def block_terms(own, own_rows, own_cols, taken, taken_rows, taken_cols, blocked, row_blocks):
    own_terms = jnp.einsum(
        "nab,nbk->nak", own, blocked[own_cols], preferred_element_type=jnp.float32
    )
    taken_terms = jnp.einsum(
        "nab,nak->nbk", taken, blocked[taken_cols], preferred_element_type=jnp.float32
    )
    return jax.ops.segment_sum(own_terms, own_rows, row_blocks) + jax.ops.segment_sum(
        taken_terms, taken_rows, row_blocks
    )


def local(embed, tiles, tile_rows, tile_cols, chg_tiles, chg_rows, chg_cols):
    rows_dev, feature_width = embed.shape
    tile_size = tiles.shape[1]
    row_count = lax.axis_size("row")
    col_count = lax.axis_size("col")
    devices = row_count * col_count
    row_blocks = rows_dev * col_count // tile_size
    col_blocks = rows_dev * row_count // tile_size
    sub_rows = rows_dev // devices
    owners = chg_cols // row_blocks * col_count + chg_rows // col_blocks
    position = jnp.arange(owners.shape[0], dtype=jnp.int32)
    earlier = position[None, :] < position[:, None]
    slot_rank = jnp.sum(jnp.logical_and(owners[:, None] == owners[None, :], earlier), axis=1)
    outgoing = (
        jnp.zeros((devices, CAP, tile_size, tile_size), jnp.bfloat16)
        .at[owners, slot_rank]
        .set(chg_tiles)
    )
    placing = jnp.stack([chg_cols % row_blocks, chg_rows % col_blocks], axis=1)
    output_slots = jnp.zeros((devices, CAP, 2), jnp.int32).at[owners, slot_rank].set(placing)
    taken, taken_places = (
        lax.all_to_all(outgoing, ("row", "col"), split_axis=0, concat_axis=0, tiled=True),
        lax.all_to_all(output_slots, ("row", "col"), split_axis=0, concat_axis=0, tiled=True),
    )
    taken = taken.reshape(devices * CAP, tile_size, tile_size)
    taken_places = taken_places.reshape(devices * CAP, 2)
    taken_rows = taken_places[:, 0]
    taken_cols = taken_places[:, 1]
    own_rows = tile_rows % row_blocks
    own_cols = tile_cols % col_blocks
    degree_terms = jax.ops.segment_sum(
        jnp.sum(jnp.abs(tiles), axis=2, dtype=jnp.float32), own_rows, row_blocks
    )
    degree_terms = degree_terms + jax.ops.segment_sum(
        jnp.sum(jnp.abs(taken), axis=1, dtype=jnp.float32), taken_rows, row_blocks
    )
    degree = 1.0 + lax.psum_scatter(
        degree_terms.astype(jnp.bfloat16), "col", scatter_dimension=0, tiled=True
    ).astype(jnp.float32).reshape(rows_dev, 1)
    nodes = rows_dev * devices
    current = embed
    final_output = embed.astype(jnp.float32)
    for iteration in range(ITERS):
        received_terms = lax.all_to_all(
            current.reshape(devices, sub_rows, feature_width),
            ("row", "col"),
            split_axis=0,
            concat_axis=0,
            tiled=True,
        )
        group = lax.all_gather(
            received_terms.reshape(rows_dev, feature_width), "row", axis=0, tiled=True
        )
        blocked = group.reshape(col_blocks, tile_size, feature_width)
        partial_value = block_terms(
            tiles, own_rows, own_cols, taken, taken_rows, taken_cols, blocked, row_blocks
        )
        summed = lax.psum_scatter(
            partial_value.reshape(row_blocks * tile_size, feature_width).astype(jnp.bfloat16),
            "col",
            scatter_dimension=0,
            tiled=True,
        ).astype(jnp.float32)
        scaled = summed / degree
        local_gram = jnp.dot(
            scaled.T, scaled, precision=lax.Precision.HIGHEST, preferred_element_type=jnp.float32
        )
        gram = lax.psum(local_gram, ("row", "col")) / nodes
        lower = jnp.linalg.cholesky(gram)
        final_output = lax.linalg.triangular_solve(
            lower, scaled, left_side=False, lower=True, transpose_a=True
        )
        current = final_output.astype(jnp.bfloat16)
    return final_output


def solution(mesh):
    placed = (
        P(("row", "col"), None),
        P(("row", "col"), None, None),
        P(("row", "col")),
        P(("row", "col")),
        P(("row", "col"), None, None),
        P(("row", "col")),
        P(("row", "col")),
    )
    return jax.shard_map(
        local, mesh=mesh, in_specs=placed, out_specs=P(("row", "col"), None), check_vma=False
    )
```

profile of v0, /device:TPU:1, one launch (start us, length us, event | category | flops | bytes accessed | tf_op | source)
XLA Modules:
  0.0 1204.5 jit_solution(14980614209809009102)
XLA Ops:
  8.4 10.1 scatter_fusion.1
  18.5 1.5 copy.79
  20.0 11.5 all-to-all-start.1
  31.6 1.2 copy.75
  33.8 7.8 all-to-all-done.1
  41.6 4.1 all-to-all-start
  45.7 7.7 broadcast_in_dim.14
  53.4 30.8 %scatter_fusion.2 = bf16[128,3,128,128]{3,2,1,0:T(8,128)(2,1)} fusion(bf16[128,3,128,128]{3,2,1,0:T(8,128)(2,1)} %broadcast_in_dim.14, s32[192]{0:T(256)S(1)} %bitcast.91, bf16[192,128,128]{2,1,0:T(8,128)(2,1)} %param.14), kind=kCustom, calls=%fused_computation.8 | custom fusion | bytes 18875904 | tf_op jit(solution)/shard_map/scatter | solution.py:38
  84.2 10.2 all-to-all-start.2
  94.5 1.1 reshape.236
  97.6 142.3 %all-gather.4.cloned.1.call-done = bf16[16384,64]{1,0:T(8,128)(2,1)} async-done(((bf16[2048,64]{1,0:T(8,128)(2,1)}), bf16[16384,64]{1,0:T(8,128)(2,1)}) %all-gather.4.cloned.1.call-update) | async-done | bytes 2097168 | tf_op jit(solution)/shard_map/all_gather | solution.py:72
  239.9 3.9 copy.77
  243.8 13.3 %gather_fusion.1 = bf16[384,128,64]{1,2,0:T(8,128)(2,1)} fusion(bf16[128,128,64]{1,2,0:T(8,128)(2,1)S(1)} %copy.77, s32[1024]{0:T(1024)S(1)} %pad_clamp_fusion), kind=kCustom, calls=%fused_computation.1 | custom fusion | bytes 12584448 | tf_op jit(solution)/shard_map/gather | solution.py:15
  257.8 3.1 convolution_bitcast_fusion.5
  260.9 4.3 broadcast.110.clone.2
  265.2 9.0 scatter_fusion
  274.2 9.2 convert_reduce_fusion
  283.5 2.5 scatter_custom_fusion.5
  286.7 14.3 %fusion.38 = f32[384,128,64]{1,2,0:T(8,128)} fusion(bf16[384,128,64]{1,2,0:T(8,128)(2,1)} %gather_fusion.1, bf16[384,128,128]{2,1,0:T(8,128)(2,1)} %bitcast.9), kind=kOutput, calls=%fused_computation.120 | convolution fusion | flops 805306368 | bytes 31457280 | tf_op jit(solution)/shard_map/nab,nak->nbk/dot_general | solution.py:14
  301.0 4.3 broadcast.110.clone.3
  305.3 59.8 %scatter_fusion.3 = f32[256,128,64]{1,2,0:T(8,128)} fusion(f32[256,128,64]{1,2,0:T(8,128)} %broadcast.110.clone.3, s32[384]{0:T(512)S(1)} %get-tuple-element.8, f32[384,128,64]{1,2,0:T(8,128)} %fusion.38), kind=kCustom, calls=%fused_computation.9 | custom fusion | flops 3145728 | bytes 37750272 | tf_op jit(solution)/shard_map/scatter-add | solution.py:17
  365.1 8.6 copy_bitcast_fusion.2
  375.0 8.3 all-reduce.3.cloned.1.call-done
  384.0 84.0 %reduce-scatter.4.cloned.1.call-done = bf16[2048,64]{0,1:T(8,128)(2,1)} async-done(((bf16[32768,64]{0,1:T(8,128)(2,1)}), bf16[2048,64]{0,1:T(8,128)(2,1)}) %reduce-scatter.4.cloned.1.call-update) | async-done | bytes 262160 | tf_op jit(solution)/shard_map/reduce_scatter | solution.py:79
  468.0 1.7 fusion.5
  469.7 66.1 %psum.21 = f32[64,64]{0,1:T(8,128)S(1)} all-reduce(f32[64,64]{0,1:T(8,128)S(1)} %fusion.5), channel_id=1, replica_groups=mesh['row'=8,'col'=16] {'row','col'}, use_global_device_ids=true, to_apply=%region_11.12 | all-reduce | flops 4096 | bytes 32768 | tf_op jit(solution)/shard_map/psum | solution.py:89
  535.9 5.8 cholesky.59
  543.1 4.9 custom-call.11
  548.0 1.6 fusion.3
  550.2 15.7 %all_to_all.25 = bf16[128,2,512]{2,1,0:T(2,128)(2,1)S(1)} all-to-all(bf16[128,2,512]{2,1,0:T(2,128)(2,1)S(1)} %reshape.237), channel_id=1, replica_groups=mesh['row'=8,'col'=16] {'row','col'}, dimensions={0} | all-to-all | bytes 524288 | tf_op jit(solution)/shard_map/all_to_all | solution.py:65
  565.9 1.1 reshape.238
  567.3 28.7 %all-gather.6.cloned.1.call-done = bf16[16384,64]{1,0:T(8,128)(2,1)} async-done(((bf16[2048,64]{1,0:T(8,128)(2,1)}), bf16[16384,64]{1,0:T(8,128)(2,1)}) %all-gather.6.cloned.1.call-update) | async-done | bytes 2097168 | tf_op jit(solution)/shard_map/all_gather | solution.py:72
  595.9 3.7 copy.87
  599.6 13.3 %gather_fusion.3 = bf16[384,128,64]{1,2,0:T(8,128)(2,1)} fusion(bf16[128,128,64]{1,2,0:T(8,128)(2,1)S(1)} %copy.87, s32[1024]{0:T(1024)S(1)} %pad_clamp_fusion), kind=kCustom, calls=%fused_computation.3 | custom fusion | bytes 12584448 | tf_op jit(solution)/shard_map/gather | solution.py:15
  613.7 14.4 %fusion.39 = f32[384,128,64]{1,2,0:T(8,128)} fusion(bf16[384,128,64]{1,2,0:T(8,128)(2,1)} %gather_fusion.3, bf16[384,128,128]{2,1,0:T(8,128)(2,1)} %bitcast.9), kind=kOutput, calls=%fused_computation.121 | convolution fusion | flops 805306368 | bytes 31457280 | tf_op jit(solution)/shard_map/nab,nak->nbk/dot_general | solution.py:14
  628.1 1.5 convolution_bitcast_fusion.4
  629.6 4.3 broadcast.110.clone.4
  633.9 59.8 %scatter_fusion.5 = f32[256,128,64]{1,2,0:T(8,128)} fusion(f32[256,128,64]{1,2,0:T(8,128)} %broadcast.110.clone.4, s32[384]{0:T(512)S(1)} %get-tuple-element.8, f32[384,128,64]{1,2,0:T(8,128)} %fusion.39), kind=kCustom, calls=%fused_computation.13 | custom fusion | flops 3145728 | bytes 37750272 | tf_op jit(solution)/shard_map/scatter-add | solution.py:17
  693.7 4.3 broadcast.110.clone.1
  698.0 9.2 scatter_fusion.4
  707.2 8.6 copy_bitcast_fusion.1
  715.9 75.9 %reduce-scatter.6.cloned.1.call-done = bf16[2048,64]{0,1:T(8,128)(2,1)} async-done(((bf16[32768,64]{0,1:T(8,128)(2,1)}), bf16[2048,64]{0,1:T(8,128)(2,1)}) %reduce-scatter.6.cloned.1.call-update) | async-done | bytes 262160 | tf_op jit(solution)/shard_map/reduce_scatter | solution.py:79
  791.8 1.7 fusion.6
  793.4 66.2 %psum.22 = f32[64,64]{0,1:T(8,128)S(1)} all-reduce(f32[64,64]{0,1:T(8,128)S(1)} %fusion.6), channel_id=1, replica_groups=mesh['row'=8,'col'=16] {'row','col'}, use_global_device_ids=true, to_apply=%region_17.20 | all-reduce | flops 4096 | bytes 32768 | tf_op jit(solution)/shard_map/psum | solution.py:89
  859.7 5.8 cholesky.70
  866.9 4.9 custom-call.12
  871.8 1.6 fusion.4
  873.9 15.7 %all_to_all.26 = bf16[128,2,512]{2,1,0:T(2,128)(2,1)S(1)} all-to-all(bf16[128,2,512]{2,1,0:T(2,128)(2,1)S(1)} %reshape.239), channel_id=1, replica_groups=mesh['row'=8,'col'=16] {'row','col'}, dimensions={0} | all-to-all | bytes 524288 | tf_op jit(solution)/shard_map/all_to_all | solution.py:65
  890.9 28.8 %all-gather.8.cloned.1.call-done = bf16[16384,64]{1,0:T(8,128)(2,1)} async-done(((bf16[2048,64]{1,0:T(8,128)(2,1)}), bf16[16384,64]{1,0:T(8,128)(2,1)}) %all-gather.8.cloned.1.call-update) | async-done | bytes 2097168 | tf_op jit(solution)/shard_map/all_gather | solution.py:72
  919.7 3.7 copy.94
  923.4 13.3 %gather_fusion.5 = bf16[384,128,64]{1,2,0:T(8,128)(2,1)} fusion(bf16[128,128,64]{1,2,0:T(8,128)(2,1)S(1)} %copy.94, s32[1024]{0:T(1024)S(1)} %pad_clamp_fusion), kind=kCustom, calls=%fused_computation.5 | custom fusion | bytes 12584448 | tf_op jit(solution)/shard_map/gather | solution.py:15
  937.5 14.4 %fusion.40 = f32[384,128,64]{1,2,0:T(8,128)} fusion(bf16[384,128,64]{1,2,0:T(8,128)(2,1)} %gather_fusion.5, bf16[384,128,128]{2,1,0:T(8,128)(2,1)} %bitcast.9), kind=kOutput, calls=%fused_computation.122 | convolution fusion | flops 805306368 | bytes 31457280 | tf_op jit(solution)/shard_map/nab,nak->nbk/dot_general | solution.py:14
  951.9 1.5 convolution_bitcast_fusion.3
  953.4 4.3 broadcast.110.clone.5
  957.7 58.9 %scatter_fusion.7 = f32[256,128,64]{1,2,0:T(8,128)} fusion(f32[256,128,64]{1,2,0:T(8,128)} %broadcast.110.clone.5, s32[384]{0:T(512)S(1)} %get-tuple-element.8, f32[384,128,64]{1,2,0:T(8,128)} %fusion.40), kind=kCustom, calls=%fused_computation.15 | custom fusion | flops 3145728 | bytes 37750272 | tf_op jit(solution)/shard_map/scatter-add | solution.py:17
  1016.6 4.3 broadcast.110.clone
  1020.9 9.2 scatter_fusion.6
  1030.1 8.5 copy_bitcast_fusion
  1038.7 75.5 %reduce-scatter.8.cloned.1.call-done = bf16[2048,64]{0,1:T(8,128)(2,1)} async-done(((bf16[32768,64]{0,1:T(8,128)(2,1)}), bf16[2048,64]{0,1:T(8,128)(2,1)}) %reduce-scatter.8.cloned.1.call-update) | async-done | bytes 262160 | tf_op jit(solution)/shard_map/reduce_scatter | solution.py:79
  1114.2 1.7 fusion.7
  1115.9 66.3 %psum.23 = f32[64,64]{0,1:T(8,128)S(1)} all-reduce(f32[64,64]{0,1:T(8,128)S(1)} %fusion.7), channel_id=1, replica_groups=mesh['row'=8,'col'=16] {'row','col'}, use_global_device_ids=true, to_apply=%region_21.24 | all-reduce | flops 4096 | bytes 32768 | tf_op jit(solution)/shard_map/psum | solution.py:89
  1182.2 5.8 cholesky.81
  1189.4 4.9 custom-call.13
  1194.3 2.4 convolution_bitcast_fusion
  (74 shorter events, 15.2 us)
Async XLA Ops:
  20.0 21.6 %all-to-all-start.1 = ((s32[128,3,2]{1,2,0:T(2,128)}), s32[128,3,2]{1,2,0:T(2,128)S(1)}, u32[]{:S(2)}, u32[]{:S(2)}) async-start(s32[128,3,2]{1,2,0:T(2,128)} %copy.79), calls=%async_computation.1 | async-start | bytes 262144 | tf_op jit(solution)/shard_map/all_to_all | solution.py:44
  41.6 42.6 %all-to-all-start = ((bf16[128,2,512]{2,1,0:T(2,128)(2,1)}), bf16[128,2,512]{2,1,0:T(2,128)(2,1)S(1)}, u32[]{:S(2)}, u32[]{:S(2)}) async-start(bf16[128,2,512]{2,1,0:T(2,128)(2,1)} %reshape.235), calls=%async_computation | async-start | bytes 524288 | tf_op jit(solution)/shard_map/all_to_all | solution.py:65
  84.2 11.5 copy-start.3
  84.2 11.6 copy-start
  84.2 13.1 %copy-start.4 = (s32[64]{0:T(128)S(1)}, s32[64]{0:T(128)}, u32[]{:S(2)}) copy-start(s32[64]{0:T(128)} %param.13) | copy-start | bytes 772
  84.2 190.0 %all-to-all-start.2 = ((bf16[128,3,128,128]{3,2,1,0:T(8,128)(2,1)}), bf16[128,3,128,128]{3,2,1,0:T(8,128)(2,1)}, u32[]{:S(2)}, u32[]{:S(2)}) async-start(bf16[128,3,128,128]{3,2,1,0:T(8,128)(2,1)} %scatter_fusion.2), calls=%async_computation.2 | async-start | bytes 25165824 | tf_op jit(solution)/shard_map/all_to_all | solution.py:43
  94.5 145.4 %all-gather.4.cloned.1.call-start = ((), (), s32[]{:S(2)}) async-start(), calls=%async_computation.8 | async-start | bytes 4718592 | tf_op jit(solution)/shard_map/all_gather | solution.py:72
  95.7 287.6 %all-reduce.3.cloned.1.call-start = ((), (), s32[]{:S(2)}) async-start(), calls=%async_computation.14 | async-start | bytes 131072
  286.7 181.4 %reduce-scatter.4.cloned.1.call-start = ((), (), s32[]{:S(2)}) async-start(), calls=%async_computation.9 | async-start | bytes 4456448 | tf_op jit(solution)/shard_map/reduce_scatter | solution.py:79
  365.1 8.7 copy-start.5
  373.7 222.2 %all-gather.6.cloned.1.call-start = ((), (), s32[]{:S(2)}) async-start(), calls=%async_computation.10 | async-start | bytes 4718592 | tf_op jit(solution)/shard_map/all_gather | solution.py:72
  567.1 224.7 %reduce-scatter.6.cloned.1.call-start = ((), (), s32[]{:S(2)}) async-start(), calls=%async_computation.11 | async-start | bytes 4456448 | tf_op jit(solution)/shard_map/reduce_scatter | solution.py:79
  613.7 14.4 %copy-start.1 = (bf16[64,128,128]{2,1,0:T(8,128)(2,1)S(1)}, bf16[64,128,128]{2,1,0:T(8,128)(2,1)}, u32[]{:S(2)}) copy-start(bf16[64,128,128]{2,1,0:T(8,128)(2,1)} %param.11) | copy-start | bytes 6291460
  715.8 203.9 %all-gather.8.cloned.1.call-start = ((), (), s32[]{:S(2)}) async-start(), calls=%async_computation.12 | async-start | bytes 4718592 | tf_op jit(solution)/shard_map/all_gather | solution.py:72
  890.8 223.4 %reduce-scatter.8.cloned.1.call-start = ((), (), s32[]{:S(2)}) async-start(), calls=%async_computation.13 | async-start | bytes 4456448 | tf_op jit(solution)/shard_map/reduce_scatter | solution.py:79
  937.5 14.4 %copy-start.2 = (bf16[64,128,128]{2,1,0:T(8,128)(2,1)S(1)}, bf16[64,128,128]{2,1,0:T(8,128)(2,1)}, u32[]{:S(2)}) copy-start(bf16[64,128,128]{2,1,0:T(8,128)(2,1)} %param.11) | copy-start | bytes 6291460
Sparse Core Ops, SparseCore 0:
  97.1 142.6 all-gather.3
  567.2 28.7 all-gather.5
  891.0 28.7 all-gather.7
Sparse Core Ops, SparseCore 1:
  286.7 96.5 all-reduce.2
  386.9 81.1 reduce-scatter.3
  715.9 75.8 reduce-scatter.5
  1038.8 75.4 reduce-scatter.7
where the time goes:
time: 1210 us; the launch traced here: 1200 us
  waiting for transfers between devices  451 us (37%)
  other arithmetic  283 us (23%)
  blocking collectives  230 us (19%)
  local copies, waits for them, and re-layouts  137 us (11%)
  matrix products  59.8 us (5%)
  starting transfers between devices  26.3 us (2%)
  between operations  16.4 us (1%)
    reduce_scatter x3, waiting for transfers between devices, local(): lax.psum_scatter(partial_value.reshape(row_blocks * tile_size, feature_wi...  235 us
    all_gather x3, waiting for transfers between devices, local(): lax.all_gather(received_terms.reshape(rows_dev, feature_width), 'row', ax...  200 us
    psum x3, blocking collectives, local(): gram = lax.psum(local_gram, ('row', 'col')) / nodes  199 us
    scatter-add x3, other arithmetic, block_terms(): jax.ops.segment_sum(taken_terms, taken_rows, row_blocks)  179 us
    dot_general x3, matrix products, block_terms(): jnp.einsum('nab,nak->nbk', taken, blocked[taken_cols], preferred_element_...  43.1 us
    gather x3, local copies, waits for them, and re-layouts, block_terms(): blocked[taken_cols]  39.8 us
    all_to_all x2, blocking collectives, local(): lax.all_to_all(current.reshape(devices, sub_rows, feature_width), ('row',...  31.5 us
    scatter x1, local copies, waits for them, and re-layouts, local(): outgoing = jnp.zeros((devices, CAP, tile_size, tile_size), jnp.bfloat16)....  30.8 us
  transfers between devices with their start and end apart: 10, of which 8 were waited for; matrix products, arithmetic and copies ran while one was open for 14% of the time, Pallas kernels for 0%

commit v1 on v0

--- a/solution.py
+++ b/solution.py
@@ -86,7 +86,7 @@
         local_gram = jnp.dot(
             scaled.T, scaled, precision=lax.Precision.HIGHEST, preferred_element_type=jnp.float32
         )
-        gram = lax.psum(local_gram, ("row", "col")) / nodes
+        gram = lax.psum(lax.psum(local_gram, "col"), "row") / nodes
         lower = jnp.linalg.cholesky(gram)
         final_output = lax.linalg.triangular_solve(
             lower, scaled, left_side=False, lower=True, transpose_a=True

time: 1210 us -> 1310 us (1.083)
  blocking collectives: 230 us -> 319 us
    psum x3 -> x6, blocking collectives: 199 us -> 284 us  [local(): gram = lax.psum(lax.psum(local_gram, 'col'), 'row') / nodes]
  transfers between devices with their start and end apart: 10 -> 10, of which waited for: 8 -> 8; matrix products, arithmetic and copies ran while one was open for 14% -> 13% of each run, Pallas kernels for 0% -> 0%
where the time goes in v1:
time: 1310 us; the launch traced here: 1290 us
  waiting for transfers between devices  452 us (35%)
  blocking collectives  319 us (24%)
  other arithmetic  283 us (22%)
  local copies, waits for them, and re-layouts  137 us (10%)
  matrix products  59.8 us (5%)
  starting transfers between devices  26.2 us (2%)
  between operations  16.4 us (1%)
    psum x6, blocking collectives, local(): gram = lax.psum(lax.psum(local_gram, 'col'), 'row') / nodes  284 us
    reduce_scatter x3, waiting for transfers between devices, local(): lax.psum_scatter(partial_value.reshape(row_blocks * tile_size, feature_wi...  235 us
    all_gather x3, waiting for transfers between devices, local(): lax.all_gather(received_terms.reshape(rows_dev, feature_width), 'row', ax...  200 us
    scatter-add x3, other arithmetic, block_terms(): jax.ops.segment_sum(taken_terms, taken_rows, row_blocks)  179 us
    dot_general x3, matrix products, block_terms(): jnp.einsum('nab,nak->nbk', taken, blocked[taken_cols], preferred_element_...  43.1 us
    gather x3, local copies, waits for them, and re-layouts, block_terms(): blocked[taken_cols]  39.8 us
    all_to_all x2, blocking collectives, local(): lax.all_to_all(current.reshape(devices, sub_rows, feature_width), ('row',...  35.2 us
    scatter x1, local copies, waits for them, and re-layouts, local(): outgoing = jnp.zeros((devices, CAP, tile_size, tile_size), jnp.bfloat16)....  30.8 us
  transfers between devices with their start and end apart: 10, of which 8 were waited for; matrix products, arithmetic and copies ran while one was open for 13% of the time, Pallas kernels for 0%

profile of v1, /device:TPU:1, one launch (start us, length us, event | category | flops | bytes accessed | tf_op | source)
XLA Modules:
  0.0 1293.3 jit_solution(9744508381227670489)
XLA Ops:
  8.4 10.1 scatter_fusion.1
  18.5 1.5 copy.79
  20.0 11.5 all-to-all-start.1
  33.8 7.8 all-to-all-done.1
  41.6 4.1 all-to-all-start
  45.7 7.7 broadcast_in_dim.14
  53.4 30.8 %scatter_fusion.2 = bf16[128,3,128,128]{3,2,1,0:T(8,128)(2,1)} fusion(bf16[128,3,128,128]{3,2,1,0:T(8,128)(2,1)} %broadcast_in_dim.14, s32[192]{0:T(256)S(1)} %bitcast.91, bf16[192,128,128]{2,1,0:T(8,128)(2,1)} %param.14), kind=kCustom, calls=%fused_computation.8 | custom fusion | bytes 18875904 | tf_op jit(solution)/shard_map/scatter | solution.py:38
  84.2 10.2 all-to-all-start.2
  97.6 142.3 %all-gather.4.cloned.1.call-done = bf16[16384,64]{1,0:T(8,128)(2,1)} async-done(((bf16[2048,64]{1,0:T(8,128)(2,1)}), bf16[16384,64]{1,0:T(8,128)(2,1)}) %all-gather.4.cloned.1.call-update) | async-done | bytes 2097168 | tf_op jit(solution)/shard_map/all_gather | solution.py:72
  239.9 3.9 copy.77
  243.8 13.3 %gather_fusion.1 = bf16[384,128,64]{1,2,0:T(8,128)(2,1)} fusion(bf16[128,128,64]{1,2,0:T(8,128)(2,1)S(1)} %copy.77, s32[1024]{0:T(1024)S(1)} %pad_clamp_fusion), kind=kCustom, calls=%fused_computation.1 | custom fusion | bytes 12584448 | tf_op jit(solution)/shard_map/gather | solution.py:15
  257.8 3.1 convolution_bitcast_fusion.5
  260.9 4.3 broadcast.110.clone.2
  265.2 9.0 scatter_fusion
  274.2 9.2 convert_reduce_fusion
  283.5 2.5 scatter_custom_fusion.5
  286.7 14.3 %fusion.38 = f32[384,128,64]{1,2,0:T(8,128)} fusion(bf16[384,128,64]{1,2,0:T(8,128)(2,1)} %gather_fusion.1, bf16[384,128,128]{2,1,0:T(8,128)(2,1)} %bitcast.9), kind=kOutput, calls=%fused_computation.120 | convolution fusion | flops 805306368 | bytes 31457280 | tf_op jit(solution)/shard_map/nab,nak->nbk/dot_general | solution.py:14
  301.0 4.3 broadcast.110.clone.3
  305.3 59.8 %scatter_fusion.3 = f32[256,128,64]{1,2,0:T(8,128)} fusion(f32[256,128,64]{1,2,0:T(8,128)} %broadcast.110.clone.3, s32[384]{0:T(512)S(1)} %get-tuple-element.8, f32[384,128,64]{1,2,0:T(8,128)} %fusion.38), kind=kCustom, calls=%fused_computation.9 | custom fusion | flops 3145728 | bytes 37750272 | tf_op jit(solution)/shard_map/scatter-add | solution.py:17
  365.1 8.6 copy_bitcast_fusion.2
  375.0 8.3 all-reduce.3.cloned.1.call-done
  384.0 84.0 %reduce-scatter.4.cloned.1.call-done = bf16[2048,64]{0,1:T(8,128)(2,1)} async-done(((bf16[32768,64]{0,1:T(8,128)(2,1)}), bf16[2048,64]{0,1:T(8,128)(2,1)}) %reduce-scatter.4.cloned.1.call-update) | async-done | bytes 262160 | tf_op jit(solution)/shard_map/reduce_scatter | solution.py:79
  468.0 1.7 fusion.5
  469.7 57.9 %psum.42 = f32[64,64]{0,1:T(8,128)S(1)} all-reduce(f32[64,64]{0,1:T(8,128)S(1)} %fusion.5), channel_id=1, replica_groups=mesh['row'=8,'col'=16] {'col'}, use_global_device_ids=true, to_apply=%region_11.12 | all-reduce | flops 4096 | bytes 32768 | tf_op jit(solution)/shard_map/psum | solution.py:89
  527.6 36.7 %psum.43 = f32[64,64]{0,1:T(8,128)S(1)} all-reduce(f32[64,64]{0,1:T(8,128)S(1)} %psum.42), channel_id=1, replica_groups=mesh['row'=8,'col'=16] {'row'}, use_global_device_ids=true, to_apply=%region_12.13 | all-reduce | flops 4096 | bytes 32768 | tf_op jit(solution)/shard_map/psum | solution.py:89
  564.3 5.8 cholesky.59
  571.5 4.9 custom-call.11
  576.4 1.6 fusion.3
  578.6 17.6 %all_to_all.25 = bf16[128,2,512]{2,1,0:T(2,128)(2,1)S(1)} all-to-all(bf16[128,2,512]{2,1,0:T(2,128)(2,1)S(1)} %reshape.237), channel_id=1, replica_groups=mesh['row'=8,'col'=16] {'row','col'}, dimensions={0} | all-to-all | bytes 524288 | tf_op jit(solution)/shard_map/all_to_all | solution.py:65
  597.4 28.8 %all-gather.6.cloned.1.call-done = bf16[16384,64]{1,0:T(8,128)(2,1)} async-done(((bf16[2048,64]{1,0:T(8,128)(2,1)}), bf16[16384,64]{1,0:T(8,128)(2,1)}) %all-gather.6.cloned.1.call-update) | async-done | bytes 2097168 | tf_op jit(solution)/shard_map/all_gather | solution.py:72
  626.2 3.8 copy.87
  630.1 13.3 %gather_fusion.3 = bf16[384,128,64]{1,2,0:T(8,128)(2,1)} fusion(bf16[128,128,64]{1,2,0:T(8,128)(2,1)S(1)} %copy.87, s32[1024]{0:T(1024)S(1)} %pad_clamp_fusion), kind=kCustom, calls=%fused_computation.3 | custom fusion | bytes 12584448 | tf_op jit(solution)/shard_map/gather | solution.py:15
  644.1 14.4 %fusion.39 = f32[384,128,64]{1,2,0:T(8,128)} fusion(bf16[384,128,64]{1,2,0:T(8,128)(2,1)} %gather_fusion.3, bf16[384,128,128]{2,1,0:T(8,128)(2,1)} %bitcast.9), kind=kOutput, calls=%fused_computation.121 | convolution fusion | flops 805306368 | bytes 31457280 | tf_op jit(solution)/shard_map/nab,nak->nbk/dot_general | solution.py:14
  658.6 1.5 convolution_bitcast_fusion.4
  660.1 4.3 broadcast.110.clone.4
  664.4 59.8 %scatter_fusion.5 = f32[256,128,64]{1,2,0:T(8,128)} fusion(f32[256,128,64]{1,2,0:T(8,128)} %broadcast.110.clone.4, s32[384]{0:T(512)S(1)} %get-tuple-element.8, f32[384,128,64]{1,2,0:T(8,128)} %fusion.39), kind=kCustom, calls=%fused_computation.13 | custom fusion | flops 3145728 | bytes 37750272 | tf_op jit(solution)/shard_map/scatter-add | solution.py:17
  724.2 4.3 broadcast.110.clone.1
  728.4 9.2 scatter_fusion.4
  737.7 8.6 copy_bitcast_fusion.1
  746.3 76.0 %reduce-scatter.6.cloned.1.call-done = bf16[2048,64]{0,1:T(8,128)(2,1)} async-done(((bf16[32768,64]{0,1:T(8,128)(2,1)}), bf16[2048,64]{0,1:T(8,128)(2,1)}) %reduce-scatter.6.cloned.1.call-update) | async-done | bytes 262160 | tf_op jit(solution)/shard_map/reduce_scatter | solution.py:79
  822.3 1.7 fusion.6
  823.9 57.9 %psum.44 = f32[64,64]{0,1:T(8,128)S(1)} all-reduce(f32[64,64]{0,1:T(8,128)S(1)} %fusion.6), channel_id=1, replica_groups=mesh['row'=8,'col'=16] {'col'}, use_global_device_ids=true, to_apply=%region_18.21 | all-reduce | flops 4096 | bytes 32768 | tf_op jit(solution)/shard_map/psum | solution.py:89
  881.8 36.6 %psum.45 = f32[64,64]{0,1:T(8,128)S(1)} all-reduce(f32[64,64]{0,1:T(8,128)S(1)} %psum.44), channel_id=1, replica_groups=mesh['row'=8,'col'=16] {'row'}, use_global_device_ids=true, to_apply=%region_19.22 | all-reduce | flops 4096 | bytes 32768 | tf_op jit(solution)/shard_map/psum | solution.py:89
  918.5 5.8 cholesky.70
  925.7 4.9 custom-call.12
  930.6 1.6 fusion.4
  932.7 17.6 %all_to_all.26 = bf16[128,2,512]{2,1,0:T(2,128)(2,1)S(1)} all-to-all(bf16[128,2,512]{2,1,0:T(2,128)(2,1)S(1)} %reshape.239), channel_id=1, replica_groups=mesh['row'=8,'col'=16] {'row','col'}, dimensions={0} | all-to-all | bytes 524288 | tf_op jit(solution)/shard_map/all_to_all | solution.py:65
  951.6 28.8 %all-gather.8.cloned.1.call-done = bf16[16384,64]{1,0:T(8,128)(2,1)} async-done(((bf16[2048,64]{1,0:T(8,128)(2,1)}), bf16[16384,64]{1,0:T(8,128)(2,1)}) %all-gather.8.cloned.1.call-update) | async-done | bytes 2097168 | tf_op jit(solution)/shard_map/all_gather | solution.py:72
  980.4 3.7 copy.94
  984.1 13.3 %gather_fusion.5 = bf16[384,128,64]{1,2,0:T(8,128)(2,1)} fusion(bf16[128,128,64]{1,2,0:T(8,128)(2,1)S(1)} %copy.94, s32[1024]{0:T(1024)S(1)} %pad_clamp_fusion), kind=kCustom, calls=%fused_computation.5 | custom fusion | bytes 12584448 | tf_op jit(solution)/shard_map/gather | solution.py:15
  998.1 14.4 %fusion.40 = f32[384,128,64]{1,2,0:T(8,128)} fusion(bf16[384,128,64]{1,2,0:T(8,128)(2,1)} %gather_fusion.5, bf16[384,128,128]{2,1,0:T(8,128)(2,1)} %bitcast.9), kind=kOutput, calls=%fused_computation.122 | convolution fusion | flops 805306368 | bytes 31457280 | tf_op jit(solution)/shard_map/nab,nak->nbk/dot_general | solution.py:14
  1012.6 1.5 convolution_bitcast_fusion.3
  1014.1 4.3 broadcast.110.clone.5
  1018.4 58.9 %scatter_fusion.7 = f32[256,128,64]{1,2,0:T(8,128)} fusion(f32[256,128,64]{1,2,0:T(8,128)} %broadcast.110.clone.5, s32[384]{0:T(512)S(1)} %get-tuple-element.8, f32[384,128,64]{1,2,0:T(8,128)} %fusion.40), kind=kCustom, calls=%fused_computation.15 | custom fusion | flops 3145728 | bytes 37750272 | tf_op jit(solution)/shard_map/scatter-add | solution.py:17
  1077.3 4.3 broadcast.110.clone
  1081.6 9.2 scatter_fusion.6
  1090.8 8.5 copy_bitcast_fusion
  1099.4 75.4 %reduce-scatter.8.cloned.1.call-done = bf16[2048,64]{0,1:T(8,128)(2,1)} async-done(((bf16[32768,64]{0,1:T(8,128)(2,1)}), bf16[2048,64]{0,1:T(8,128)(2,1)}) %reduce-scatter.8.cloned.1.call-update) | async-done | bytes 262160 | tf_op jit(solution)/shard_map/reduce_scatter | solution.py:79
  1174.8 1.7 fusion.7
  1176.4 57.9 %psum.46 = f32[64,64]{0,1:T(8,128)S(1)} all-reduce(f32[64,64]{0,1:T(8,128)S(1)} %fusion.7), channel_id=1, replica_groups=mesh['row'=8,'col'=16] {'col'}, use_global_device_ids=true, to_apply=%region_23.26 | all-reduce | flops 4096 | bytes 32768 | tf_op jit(solution)/shard_map/psum | solution.py:89
  1234.3 36.6 %psum.47 = f32[64,64]{0,1:T(8,128)S(1)} all-reduce(f32[64,64]{0,1:T(8,128)S(1)} %psum.46), channel_id=1, replica_groups=mesh['row'=8,'col'=16] {'row'}, use_global_device_ids=true, to_apply=%region_24.27 | all-reduce | flops 4096 | bytes 32768 | tf_op jit(solution)/shard_map/psum | solution.py:89
  1271.0 5.8 cholesky.81
  1278.2 4.9 custom-call.13
  1283.1 2.4 convolution_bitcast_fusion
  (77 shorter events, 18.5 us)
Async XLA Ops:
  20.0 21.6 %all-to-all-start.1 = ((s32[128,3,2]{1,2,0:T(2,128)}), s32[128,3,2]{1,2,0:T(2,128)S(1)}, u32[]{:S(2)}, u32[]{:S(2)}) async-start(s32[128,3,2]{1,2,0:T(2,128)} %copy.79), calls=%async_computation.1 | async-start | bytes 262144 | tf_op jit(solution)/shard_map/all_to_all | solution.py:44
  41.6 42.6 %all-to-all-start = ((bf16[128,2,512]{2,1,0:T(2,128)(2,1)}), bf16[128,2,512]{2,1,0:T(2,128)(2,1)S(1)}, u32[]{:S(2)}, u32[]{:S(2)}) async-start(bf16[128,2,512]{2,1,0:T(2,128)(2,1)} %reshape.235), calls=%async_computation | async-start | bytes 524288 | tf_op jit(solution)/shard_map/all_to_all | solution.py:65
  84.2 11.5 copy-start.3
  84.2 11.6 copy-start
  84.2 13.1 %copy-start.4 = (s32[64]{0:T(128)S(1)}, s32[64]{0:T(128)}, u32[]{:S(2)}) copy-start(s32[64]{0:T(128)} %param.13) | copy-start | bytes 772
  84.2 190.0 %all-to-all-start.2 = ((bf16[128,3,128,128]{3,2,1,0:T(8,128)(2,1)}), bf16[128,3,128,128]{3,2,1,0:T(8,128)(2,1)}, u32[]{:S(2)}, u32[]{:S(2)}) async-start(bf16[128,3,128,128]{3,2,1,0:T(8,128)(2,1)} %scatter_fusion.2), calls=%async_computation.2 | async-start | bytes 25165824 | tf_op jit(solution)/shard_map/all_to_all | solution.py:43
  94.5 145.4 %all-gather.4.cloned.1.call-start = ((), (), s32[]{:S(2)}) async-start(), calls=%async_computation.8 | async-start | bytes 4718592 | tf_op jit(solution)/shard_map/all_gather | solution.py:72
  95.7 287.6 %all-reduce.3.cloned.1.call-start = ((), (), s32[]{:S(2)}) async-start(), calls=%async_computation.14 | async-start | bytes 131072
  286.7 181.4 %reduce-scatter.4.cloned.1.call-start = ((), (), s32[]{:S(2)}) async-start(), calls=%async_computation.9 | async-start | bytes 4456448 | tf_op jit(solution)/shard_map/reduce_scatter | solution.py:79
  365.1 8.7 copy-start.5
  373.7 252.5 %all-gather.6.cloned.1.call-start = ((), (), s32[]{:S(2)}) async-start(), calls=%async_computation.10 | async-start | bytes 4718592 | tf_op jit(solution)/shard_map/all_gather | solution.py:72
  597.4 224.9 %reduce-scatter.6.cloned.1.call-start = ((), (), s32[]{:S(2)}) async-start(), calls=%async_computation.11 | async-start | bytes 4456448 | tf_op jit(solution)/shard_map/reduce_scatter | solution.py:79
  644.1 14.4 %copy-start.1 = (bf16[64,128,128]{2,1,0:T(8,128)(2,1)S(1)}, bf16[64,128,128]{2,1,0:T(8,128)(2,1)}, u32[]{:S(2)}) copy-start(bf16[64,128,128]{2,1,0:T(8,128)(2,1)} %param.11) | copy-start | bytes 6291460
  746.2 234.1 %all-gather.8.cloned.1.call-start = ((), (), s32[]{:S(2)}) async-start(), calls=%async_computation.12 | async-start | bytes 4718592 | tf_op jit(solution)/shard_map/all_gather | solution.py:72
  951.5 223.2 %reduce-scatter.8.cloned.1.call-start = ((), (), s32[]{:S(2)}) async-start(), calls=%async_computation.13 | async-start | bytes 4456448 | tf_op jit(solution)/shard_map/reduce_scatter | solution.py:79
  998.1 14.4 %copy-start.2 = (bf16[64,128,128]{2,1,0:T(8,128)(2,1)S(1)}, bf16[64,128,128]{2,1,0:T(8,128)(2,1)}, u32[]{:S(2)}) copy-start(bf16[64,128,128]{2,1,0:T(8,128)(2,1)} %param.11) | copy-start | bytes 6291460
Sparse Core Ops, SparseCore 0:
  97.1 142.6 all-gather.3
  597.5 28.7 all-gather.5
  951.6 28.7 all-gather.7
Sparse Core Ops, SparseCore 1:
  286.7 96.5 all-reduce.2
  386.9 81.1 reduce-scatter.3
  746.3 75.9 reduce-scatter.5
  1099.4 75.3 reduce-scatter.7
